TPU v7x, 512 devices: a whole 4x4x16 slice. The times are simulated.
512 devices in a mesh: dp: 8 (over y, x_lo), ctx: 64 (over z, x_hi, core).
Axes of the slice: x: 4 (x_hi: 2, x_lo: 2; x = x_hi * 2 + x_lo), y: 4, z: 16, core: 2. Of those that a mesh axis runs over, the one named last changes fastest.
Arguments:
- events: bfloat16 [8, 16384, 1024], P('dp', 'ctx'), may hold values from -6 to 6
- w_query: bfloat16 [1024, 512], replicated, may hold values from -0.1875 to 0.1875
- w_key: bfloat16 [1024, 512], replicated, may hold values from -0.1875 to 0.1875
- values: bfloat16 [8, 16384, 512], P('dp', 'ctx'), may hold values from -6 to 6
- grad_out: bfloat16 [8, 16384, 512], P('dp', 'ctx'), may hold values from -6 to 6
- lengths: int32 [8, 32], P('dp'), may hold values from 1 to 768, 16384 in all within a row
- stream_shift: int32 [8], P('dp'), may hold values from 0 to 16383
- block_keep: int32 [8, 128], P('dp'), may hold values 0 or 1
Outputs:
- attended: bfloat16 [8, 16384, 512], P('dp', 'ctx')
- grad_values: bfloat16 [8, 16384, 512], P('dp', 'ctx')
- grad_wq: bfloat16 [1024, 512], P('ctx')
- grad_wk: bfloat16 [1024, 512], P('ctx')
Inputs may be any that keep to these rules, and one draw needn't show every extreme that they name: The lengths of a stream sum to 16384; the longest is exactly 768.
All inputs are finite; a program needn't handle non-finite values. No bound on the sum of `block_keep` on one device may be relied on, other than what follows from the above.
Results may differ from a plain program's by a relative error of at most 0.011.
Values may be sent and summed in bfloat16 or wider, within the bound.
A program may use at most 64 MiB of HBM per device.

v0:
```python
import jax
import jax.numpy as jnp
from jax import lax
from jax.sharding import PartitionSpec as P

HD = 128
SPAN = 3
BLOCK = 128
MAXLEN = 768


def shifted(value, axis, steps):
    count = lax.axis_size(axis)
    pairs = [(source, (source + steps) % count) for source in range(count)]
    return lax.ppermute(value, axis, pairs)


def scores(query, key, valid, scale, alpha):
    z = jnp.einsum("qhd,khd->hqk", query, key, preferred_element_type=jnp.float32) * alpha
    sig = jax.nn.sigmoid(z)
    weight = valid[None, :, :].astype(jnp.float32) * scale
    return (z, sig, weight)


def forward_terms(query, grad, key, value, valid, scale, alpha):
    z, sig, weight = scores(query, key, valid, scale, alpha)
    att = (z * sig * weight).astype(jnp.bfloat16)
    out = jnp.einsum("hqk,khd->qhd", att, value, preferred_element_type=jnp.float32)
    dprod = jnp.einsum("qhd,khd->hqk", grad, value, preferred_element_type=jnp.float32)
    dsc = (dprod * sig * (1.0 + z * (1.0 - sig)) * weight * alpha).astype(jnp.bfloat16)
    dquery = jnp.einsum("hqk,khd->qhd", dsc, key, preferred_element_type=jnp.float32)
    return (out, dquery, att, dsc)


def backward_terms(query, grad, key, value, valid, scale, alpha):
    z, sig, weight = scores(query, key, valid, scale, alpha)
    att = (z * sig * weight).astype(jnp.bfloat16)
    dprod = jnp.einsum("qhd,khd->hqk", grad, value, preferred_element_type=jnp.float32)
    dsc = (dprod * sig * (1.0 + z * (1.0 - sig)) * weight * alpha).astype(jnp.bfloat16)
    dkey = jnp.einsum("hqk,qhd->khd", dsc, query, preferred_element_type=jnp.float32)
    dvalue = jnp.einsum("hqk,qhd->khd", att, grad, preferred_element_type=jnp.float32)
    return (dkey, dvalue)


def body(events, w_query, w_key, values, grad_out, lengths, stream_shift, block_keep):
    rows = events.shape[1]
    features = w_query.shape[1]
    nheads = features // HD
    alpha = 1.0 / HD**0.5
    scale = 1.0 / MAXLEN**0.5
    local = events[0]
    queries = jnp.dot(local, w_query, preferred_element_type=jnp.float32).astype(jnp.bfloat16)
    keys = jnp.dot(local, w_key, preferred_element_type=jnp.float32).astype(jnp.bfloat16)
    cycle_size = lax.axis_size("ctx")
    myself = lax.axis_index("ctx")
    total = rows * cycle_size
    ends = jnp.cumsum(lengths[0])
    offset = stream_shift[0]
    keep = block_keep[0]
    blocks_all = jnp.arange(keep.shape[0], dtype=jnp.int32)
    within = jnp.arange(rows, dtype=jnp.int32)

    def describe(anchor):
        anchor = jnp.remainder(anchor, cycle_size)
        position = jnp.remainder(anchor * rows + within - offset, total)
        owner = jnp.sum((position[:, None] >= ends[None, :]).astype(jnp.int32), axis=1)
        which = position // BLOCK
        kept = (
            jnp.sum(jnp.where(which[:, None] == blocks_all[None, :], keep[None, :], 0), axis=1) > 0
        )
        return (position, owner, kept)

    def mask(qinfo, kinfo):
        return (
            (qinfo[1][:, None] == kinfo[1][None, :])
            & (kinfo[0][None, :] <= qinfo[0][:, None])
            & kinfo[2][None, :]
        )

    def split(packed):
        return (
            packed[:, :features].reshape(rows, nheads, HD),
            packed[:, features:].reshape(rows, nheads, HD),
        )

    kv = jnp.concatenate([keys, values[0]], axis=1)
    qg = jnp.concatenate([queries, grad_out[0]], axis=1)
    kv_from = [None] + [shifted(kv, "ctx", step) for step in range(1, SPAN + 1)]
    qg_from = [None] + [shifted(qg, "ctx", -step) for step in range(1, SPAN + 1)]
    q_me, g_me = split(qg)
    k_me, v_me = split(kv)
    info_me = describe(myself)
    out_acc, dq_acc, att0, dsc0 = forward_terms(
        q_me, g_me, k_me, v_me, mask(info_me, info_me), scale, alpha
    )
    dk_acc = jnp.einsum("hqk,qhd->khd", dsc0, q_me, preferred_element_type=jnp.float32)
    dv_acc = jnp.einsum("hqk,qhd->khd", att0, g_me, preferred_element_type=jnp.float32)
    for step in range(1, SPAN + 1):
        k_s, v_s = split(kv_from[step])
        o, a, _, _ = forward_terms(
            q_me, g_me, k_s, v_s, mask(info_me, describe(myself - step)), scale, alpha
        )
        out_acc = out_acc + o
        dq_acc = dq_acc + a
        q_s, g_s = split(qg_from[step])
        b, c = backward_terms(
            q_s, g_s, k_me, v_me, mask(describe(myself + step), info_me), scale, alpha
        )
        dk_acc = dk_acc + b
        dv_acc = dv_acc + c
    attended = out_acc.reshape(1, rows, features).astype(jnp.bfloat16)
    grad_values = dv_acc.reshape(1, rows, features).astype(jnp.bfloat16)
    dq_b = dq_acc.reshape(rows, features).astype(jnp.bfloat16)
    dk_b = dk_acc.reshape(rows, features).astype(jnp.bfloat16)
    joined = jnp.concatenate([dq_b, dk_b], axis=1)
    terms = jnp.einsum("rd,rf->df", local, joined, preferred_element_type=jnp.float32)
    mine = lax.psum_scatter(terms, "ctx", scatter_dimension=0, tiled=True)
    mine = lax.psum(mine, "dp")
    grad_wq = mine[:, :features].astype(jnp.bfloat16)
    grad_wk = mine[:, features:].astype(jnp.bfloat16)
    return (attended, grad_values, grad_wq, grad_wk)


def solution(mesh):
    placed = (
        P("dp", "ctx", None),
        P(),
        P(),
        P("dp", "ctx", None),
        P("dp", "ctx", None),
        P("dp", None),
        P("dp"),
        P("dp", None),
    )
    return jax.shard_map(
        body,
        mesh=mesh,
        in_specs=placed,
        out_specs=(P("dp", "ctx", None), P("dp", "ctx", None), P("ctx", None), P("ctx", None)),
        check_vma=False,
    )
```

profile of v0, /device:TPU:4, one launch (start us, length us, event | category | flops | bytes accessed | tf_op | source)
XLA Modules:
  0.0 390.5 jit_solution(711006471729276778)
XLA Ops:
  7.3 1.2 copy-done
  8.5 1.5 convolution_convert_fusion.1
  10.0 1.0 pad_maximum_fusion.1
  11.0 10.8 %collective-permute-start.5 = (bf16[256,1024]{1,0:T(8,128)(2,1)S(1)}, bf16[256,1024]{1,0:T(8,128)(2,1)}, u32[]{:S(2)}, u32[]{:S(2)}) collective-permute-start(bf16[256,1024]{1,0:T(8,128)(2,1)S(1)} %pad_maximum_fusion.1), channel_id=1, source_target_pairs={{0,61},{1,62},{2,63},{3,0},{4,1},{5,2},{6,3},{7,4},{8,5},{9,6},{10... | collective-permute-start | bytes 1572872 | tf_op jit(solution)/shard_map/ppermute | solution.py:15
  21.8 2.4 collective-permute-start.4
  24.2 4.9 %collective-permute-start.3 = (bf16[256,1024]{1,0:T(8,128)(2,1)S(1)}, bf16[256,1024]{1,0:T(8,128)(2,1)}, u32[]{:S(2)}, u32[]{:S(2)}) collective-permute-start(bf16[256,1024]{1,0:T(8,128)(2,1)S(1)} %pad_maximum_fusion.1), channel_id=1, source_target_pairs={{0,63},{1,0},{2,1},{3,2},{4,3},{5,4},{6,5},{7,6},{8,7},{9,8},{10,9... | collective-permute-start | bytes 1572872 | tf_op jit(solution)/shard_map/ppermute | solution.py:15
  29.1 1.8 convolution_convert_fusion
  31.0 0.9 pad_maximum_fusion
  31.8 3.0 collective-permute-start.2
  34.8 4.8 %collective-permute-start.1 = (bf16[256,1024]{1,0:T(8,128)(2,1)}, bf16[256,1024]{1,0:T(8,128)(2,1)}, u32[]{:S(2)}, u32[]{:S(2)}) collective-permute-start(bf16[256,1024]{1,0:T(8,128)(2,1)} %pad_maximum_fusion), channel_id=1, source_target_pairs={{0,2},{1,3},{2,4},{3,5},{4,6},{5,7},{6,8},{7,9},{8,10},{9,11},{10,... | collective-permute-start | bytes 1572872 | tf_op jit(solution)/shard_map/ppermute | solution.py:15
  41.8 1.5 and_select_fusion.2
  44.4 1.0 fusion.179
  45.5 1.1 fusion.178
  46.6 2.1 collective-permute-start
  48.7 1.8 slice_bitcast_fusion
  50.4 1.8 slice_bitcast_fusion.1
  52.3 1.8 slice_bitcast_fusion.2
  54.3 1.1 copy.201
  55.4 1.1 copy.200
  56.5 1.8 slice_bitcast_fusion.3
  58.3 1.8 copy.199
  60.1 6.7 %collective-permute-done.1 = bf16[256,1024]{1,0:T(8,128)(2,1)} collective-permute-done((bf16[256,1024]{1,0:T(8,128)(2,1)}, bf16[256,1024]{1,0:T(8,128)(2,1)}, u32[]{:S(2)}, u32[]{:S(2)}) %collective-permute-start.1) | collective-permute-done | bytes 524320 | tf_op jit(solution)/shard_map/ppermute | solution.py:15
  66.8 1.8 slice_bitcast_fusion.4
  68.7 1.8 copy.198
  70.5 1.8 slice_bitcast_fusion.5
  72.3 1.8 copy.197
  74.1 2.3 convolution_multiply_fusion.9
  76.4 2.3 convolution_multiply_fusion.8
  78.7 2.3 convolution_multiply_fusion.7
  81.0 1.4 convolution_multiply_fusion.6
  82.4 1.3 convolution_multiply_fusion.5
  83.7 1.3 convolution_multiply_fusion.4
  85.0 2.9 fusion.36
  87.9 2.9 fusion.35
  90.7 2.9 fusion.37
  93.7 2.9 fusion.42
  96.6 3.2 fusion.49
  99.8 3.2 fusion.52
  103.0 3.7 convolution_bitcast_fusion
  106.7 5.3 %copy.193 = f32[1024,1024]{1,0:T(8,128)} copy(f32[1024,1024]{0,1:T(8,128)} %convolution_bitcast_fusion) | data formatting | bytes 8388608
  113.1 1.8 convolution_bitcast_fusion.8
  115.9 0.8 copy.186
  116.7 1.9 convolution_bitcast_fusion.5
  118.7 1.4 convolution_bitcast_fusion.6
  120.6 0.8 copy.187
  121.5 217.4 %reduce-scatter.4.cloned.1.call-done = f32[16,1024]{1,0:T(8,128)} async-done(((f32[1024,1024]{1,0:T(8,128)}), f32[16,1024]{1,0:T(8,128)}) %reduce-scatter.4.cloned.1.call-update) | async-done | bytes 65552
  338.8 1.0 copy.194
  339.9 42.3 %psum.7 = bf16[16,1024]{0,1:T(8,128)(2,1)S(1)} all-reduce(f32[16,1024]{0,1:T(8,128)S(1)} %copy.194), channel_id=1, replica_groups=mesh['dp'=8,'ctx'=64] {'dp'}, use_global_device_ids=true, to_apply=%region_13.14 | all-reduce | flops 16384 | bytes 98304 | tf_op jit(solution)/shard_map/psum | solution.py:118
  (86 shorter events, 6.5 us)
Async XLA Ops:
  7.2 1.3 copy-start
  7.2 32.6 %copy-start.7 = (bf16[1,256,512]{2,1,0:T(8,128)(2,1)S(1)}, bf16[1,256,512]{2,1,0:T(8,128)(2,1)}, u32[]{:S(2)}) copy-start(bf16[1,256,512]{2,1,0:T(8,128)(2,1)} %param.12) | copy-start | bytes 786436
  7.2 23.8 %copy-start.6 = (bf16[1,256,512]{2,1,0:T(8,128)(2,1)S(1)}, bf16[1,256,512]{2,1,0:T(8,128)(2,1)}, u32[]{:S(2)}) copy-start(bf16[1,256,512]{2,1,0:T(8,128)(2,1)} %param.11) | copy-start | bytes 786436
  7.2 33.7 %copy-start.23 = (s32[1,128]{1,0:T(1,128)S(1)}, s32[1,128]{1,0:T(1,128)}, u32[]{:S(2)}) copy-start(s32[1,128]{1,0:T(1,128)} %param.15) | copy-start | bytes 1540
  7.2 34.2 %copy-start.24 = (s32[1,32]{1,0:T(1,128)S(1)}, s32[1,32]{1,0:T(1,128)}, u32[]{:S(2)}) copy-start(s32[1,32]{1,0:T(1,128)} %param.13) | copy-start | bytes 388
  7.2 331.6 %reduce-scatter.4.cloned.1.call-start = ((), (), s32[]{:S(2)}) async-start(), calls=%async_computation.1 | async-start | bytes 4259840
  11.0 35.6 %collective-permute-start.5 = (bf16[256,1024]{1,0:T(8,128)(2,1)S(1)}, bf16[256,1024]{1,0:T(8,128)(2,1)}, u32[]{:S(2)}, u32[]{:S(2)}) collective-permute-start(bf16[256,1024]{1,0:T(8,128)(2,1)S(1)} %pad_maximum_fusion.1), channel_id=1, source_target_pairs={{0,61},{1,62},{2,63},{3,0},{4,1},{5,2},{6,3},{7,4},{8,5},{9,6},{10... | collective-permute-start | bytes 1572872 | tf_op jit(solution)/shard_map/ppermute | solution.py:15
  21.8 28.6 %collective-permute-start.4 = (bf16[256,1024]{1,0:T(8,128)(2,1)S(1)}, bf16[256,1024]{1,0:T(8,128)(2,1)}, u32[]{:S(2)}, u32[]{:S(2)}) collective-permute-start(bf16[256,1024]{1,0:T(8,128)(2,1)S(1)} %pad_maximum_fusion.1), channel_id=1, source_target_pairs={{0,62},{1,63},{2,0},{3,1},{4,2},{5,3},{6,4},{7,5},{8,6},{9,7},{10,... | collective-permute-start | bytes 1572872 | tf_op jit(solution)/shard_map/ppermute | solution.py:15
  24.2 28.0 %collective-permute-start.3 = (bf16[256,1024]{1,0:T(8,128)(2,1)S(1)}, bf16[256,1024]{1,0:T(8,128)(2,1)}, u32[]{:S(2)}, u32[]{:S(2)}) collective-permute-start(bf16[256,1024]{1,0:T(8,128)(2,1)S(1)} %pad_maximum_fusion.1), channel_id=1, source_target_pairs={{0,63},{1,0},{2,1},{3,2},{4,3},{5,4},{6,5},{7,6},{8,7},{9,8},{10,9... | collective-permute-start | bytes 1572872 | tf_op jit(solution)/shard_map/ppermute | solution.py:15
  31.8 24.6 %collective-permute-start.2 = (bf16[256,1024]{1,0:T(8,128)(2,1)}, bf16[256,1024]{1,0:T(8,128)(2,1)}, u32[]{:S(2)}, u32[]{:S(2)}) collective-permute-start(bf16[256,1024]{1,0:T(8,128)(2,1)} %pad_maximum_fusion), channel_id=1, source_target_pairs={{0,3},{1,4},{2,5},{3,6},{4,7},{5,8},{6,9},{7,10},{8,11},{9,12},{10... | collective-permute-start | bytes 1572872 | tf_op jit(solution)/shard_map/ppermute | solution.py:15
  34.8 32.0 %collective-permute-start.1 = (bf16[256,1024]{1,0:T(8,128)(2,1)}, bf16[256,1024]{1,0:T(8,128)(2,1)}, u32[]{:S(2)}, u32[]{:S(2)}) collective-permute-start(bf16[256,1024]{1,0:T(8,128)(2,1)} %pad_maximum_fusion), channel_id=1, source_target_pairs={{0,2},{1,3},{2,4},{3,5},{4,6},{5,7},{6,8},{7,9},{8,10},{9,11},{10,... | collective-permute-start | bytes 1572872 | tf_op jit(solution)/shard_map/ppermute | solution.py:15
  46.6 23.9 %collective-permute-start = (bf16[256,1024]{1,0:T(8,128)(2,1)}, bf16[256,1024]{1,0:T(8,128)(2,1)}, u32[]{:S(2)}, u32[]{:S(2)}) collective-permute-start(bf16[256,1024]{1,0:T(8,128)(2,1)} %pad_maximum_fusion), channel_id=1, source_target_pairs={{0,1},{1,2},{2,3},{3,4},{4,5},{5,6},{6,7},{7,8},{8,9},{9,10},{10,1... | collective-permute-start | bytes 1572872 | tf_op jit(solution)/shard_map/ppermute | solution.py:15
  83.7 4.2 %copy-start.14 = (f32[256,256]{1,0:T(8,128)S(1)}, f32[256,256]{1,0:T(8,128)}, u32[]{:S(2)}) copy-start(f32[256,256]{1,0:T(8,128)} %get-tuple-element.47) | copy-start | bytes 786436
  87.9 2.9 copy-start.8
  90.7 3.0 copy-start.10
  90.7 3.0 copy-start.12
  93.7 2.9 copy-start.9
  96.6 3.2 copy-start.11
  99.8 3.2 copy-start.1
  112.0 0.9 copy-start.18
  112.0 1.0 copy-start.20
  112.0 2.8 copy-start.5
  112.1 2.8 copy-start.17
  112.1 2.8 copy-start.21
  113.0 2.3 copy-start.4
  113.0 2.3 copy-start.16
  113.0 2.3 copy-start.22
  115.8 2.8 copy-start.3
  115.8 2.8 copy-start.15
  116.7 3.4 copy-start.2
  116.7 3.4 copy-start.13
  116.7 3.4 copy-start.19
Sparse Core Ops, SparseCore 0:
  112.2 226.6 reduce-scatter.3
where the time goes:
time: 392 us; the launch traced here: 390 us
  waiting for transfers between devices  224 us (57%)
  matrix products  46.2 us (12%)
  blocking collectives  42.3 us (11%)
  local copies, waits for them, and re-layouts  30.3 us (8%)
  starting transfers between devices  28 us (7%)
  between operations  15.3 us (4%)
  other arithmetic  4.22 us (1%)
    unnamed x2, waiting for transfers between devices  217 us
    psum x1, blocking collectives, body(): mine = lax.psum(mine, 'dp')  42.3 us
    ppermute x6, starting transfers between devices, shifted(): return lax.ppermute(value, axis, pairs)  28 us
    unnamed x62, local copies, waits for them, and re-layouts  22.1 us
    dot_general x7, matrix products, scores(): jnp.einsum('qhd,khd->hqk', query, key, preferred_element_type=jnp.float32)  11.5 us
    dot_general x4, matrix products, forward_terms(): jnp.einsum('hqk,khd->qhd', dsc, key, preferred_element_type=jnp.float32)  10.1 us
    dot_general x3, matrix products, backward_terms(): jnp.einsum('hqk,qhd->khd', dsc, query, preferred_element_type=jnp.float32)  8.86 us
    reshape x8, local copies, waits for them, and re-layouts, split(): packed[:, :features].reshape(rows, nheads, HD)  7.94 us
  transfers between devices with their start and end apart: 7, of which 2 were waited for; matrix products, arithmetic and copies ran while one was open for 8% of the time, Pallas kernels for 0%

commit v1 on v0

--- a/solution.py
+++ b/solution.py
@@ -115,7 +115,8 @@
     joined = jnp.concatenate([dq_b, dk_b], axis=1)
     terms = jnp.einsum("rd,rf->df", local, joined, preferred_element_type=jnp.float32)
     mine = lax.psum_scatter(terms, "ctx", scatter_dimension=0, tiled=True)
-    mine = lax.psum(mine, "dp")
+    long_array = lax.all_gather(mine, axis_name="dp")
+    mine = jnp.sum(long_array, axis=0)
     grad_wq = mine[:, :features].astype(jnp.bfloat16)
     grad_wk = mine[:, features:].astype(jnp.bfloat16)
     return (attended, grad_values, grad_wq, grad_wk)

time: 392 us -> 378 us (0.964)
  the two profiles are of different devices: /device:TPU:4 before, /device:TPU:2 now
where the time goes in v1:
time: 378 us; the launch traced here: 377 us
  waiting for transfers between devices  226 us (60%)
  matrix products  45.8 us (12%)
  blocking collectives  29.8 us (8%)
  local copies, waits for them, and re-layouts  28.1 us (7%)
  starting transfers between devices  27.3 us (7%)
  between operations  15.4 us (4%)
  other arithmetic  4.24 us (1%)
    reduce_scatter x1, waiting for transfers between devices, body(): mine = lax.psum_scatter(terms, 'ctx', scatter_dimension=0, tiled=True)  219 us
    all_gather x1, blocking collectives, body(): long_array = lax.all_gather(mine, axis_name='dp')  29.8 us
    ppermute x6, starting transfers between devices, shifted(): return lax.ppermute(value, axis, pairs)  27.2 us
    unnamed x65, local copies, waits for them, and re-layouts  19.3 us
    dot_general x7, matrix products, scores(): jnp.einsum('qhd,khd->hqk', query, key, preferred_element_type=jnp.float32)  11.5 us
    dot_general x4, matrix products, forward_terms(): jnp.einsum('hqk,khd->qhd', dsc, key, preferred_element_type=jnp.float32)  10.1 us
    dot_general x3, matrix products, backward_terms(): jnp.einsum('hqk,qhd->khd', dsc, query, preferred_element_type=jnp.float32)  8.85 us
    reshape x8, local copies, waits for them, and re-layouts, split(): packed[:, :features].reshape(rows, nheads, HD)  7.94 us
  transfers between devices with their start and end apart: 7, of which 2 were waited for; matrix products, arithmetic and copies ran while one was open for 9% of the time, Pallas kernels for 0%

profile of v1, /device:TPU:2, one launch (start us, length us, event | category | flops | bytes accessed | tf_op | source)
XLA Modules:
  0.0 376.5 jit_solution(8356875037157081708)
XLA Ops:
  7.3 1.2 copy-done
  8.5 1.5 convolution_convert_fusion.1
  10.0 1.0 pad_maximum_fusion.1
  11.0 10.8 %collective-permute-start.5 = (bf16[256,1024]{1,0:T(8,128)(2,1)S(1)}, bf16[256,1024]{1,0:T(8,128)(2,1)}, u32[]{:S(2)}, u32[]{:S(2)}) collective-permute-start(bf16[256,1024]{1,0:T(8,128)(2,1)S(1)} %pad_maximum_fusion.1), channel_id=1, source_target_pairs={{0,61},{1,62},{2,63},{3,0},{4,1},{5,2},{6,3},{7,4},{8,5},{9,6},{10... | collective-permute-start | bytes 1572872 | tf_op jit(solution)/shard_map/ppermute | solution.py:15
  21.8 4.5 %collective-permute-start.4 = (bf16[256,1024]{1,0:T(8,128)(2,1)S(1)}, bf16[256,1024]{1,0:T(8,128)(2,1)}, u32[]{:S(2)}, u32[]{:S(2)}) collective-permute-start(bf16[256,1024]{1,0:T(8,128)(2,1)S(1)} %pad_maximum_fusion.1), channel_id=1, source_target_pairs={{0,62},{1,63},{2,0},{3,1},{4,2},{5,3},{6,4},{7,5},{8,6},{9,7},{10,... | collective-permute-start | bytes 1572872 | tf_op jit(solution)/shard_map/ppermute | solution.py:15
  26.3 4.9 %collective-permute-start.3 = (bf16[256,1024]{1,0:T(8,128)(2,1)S(1)}, bf16[256,1024]{1,0:T(8,128)(2,1)}, u32[]{:S(2)}, u32[]{:S(2)}) collective-permute-start(bf16[256,1024]{1,0:T(8,128)(2,1)S(1)} %pad_maximum_fusion.1), channel_id=1, source_target_pairs={{0,63},{1,0},{2,1},{3,2},{4,3},{5,4},{6,5},{7,6},{8,7},{9,8},{10,9... | collective-permute-start | bytes 1572872 | tf_op jit(solution)/shard_map/ppermute | solution.py:15
  31.2 1.8 convolution_convert_fusion
  33.0 0.9 pad_maximum_fusion
  33.9 1.9 collective-permute-start.2
  35.8 3.0 collective-permute-start.1
  41.1 1.5 and_select_fusion.2
  43.7 1.0 fusion.179
  44.7 1.1 fusion.178
  45.9 2.1 collective-permute-start
  48.0 1.8 slice_bitcast_fusion
  49.7 1.8 slice_bitcast_fusion.1
  51.6 1.8 slice_bitcast_fusion.2
  53.5 1.1 copy.196
  54.6 1.1 copy.195
  55.7 1.8 slice_bitcast_fusion.3
  57.6 1.8 copy.194
  59.4 6.5 %collective-permute-done.1 = bf16[256,1024]{1,0:T(8,128)(2,1)} collective-permute-done((bf16[256,1024]{1,0:T(8,128)(2,1)}, bf16[256,1024]{1,0:T(8,128)(2,1)}, u32[]{:S(2)}, u32[]{:S(2)}) %collective-permute-start.1) | collective-permute-done | bytes 524320 | tf_op jit(solution)/shard_map/ppermute | solution.py:15
  65.9 1.8 slice_bitcast_fusion.4
  67.7 1.8 copy.193
  69.5 1.8 slice_bitcast_fusion.5
  71.4 1.8 copy.192
  73.2 2.3 convolution_multiply_fusion.9
  75.4 2.3 convolution_multiply_fusion.8
  77.8 2.3 convolution_multiply_fusion.7
  80.0 1.4 convolution_multiply_fusion.6
  81.4 1.3 convolution_multiply_fusion.5
  82.7 1.3 convolution_multiply_fusion.4
  84.1 2.9 fusion.36
  87.0 2.8 fusion.35
  89.8 3.0 fusion.37
  92.8 2.9 fusion.42
  95.7 3.2 fusion.49
  98.9 3.1 fusion.52
  102.0 3.7 convolution_bitcast_fusion
  105.7 5.3 %copy.188 = f32[1024,1024]{1,0:T(8,128)} copy(f32[1024,1024]{0,1:T(8,128)} %convolution_bitcast_fusion) | data formatting | bytes 8388608
  111.1 1.1 convolution_bitcast_fusion.4
  112.6 1.8 convolution_bitcast_fusion.8
  115.4 0.8 copy.183
  116.3 1.6 convolution_bitcast_fusion.5
  119.0 0.8 copy.184
  119.8 219.4 %reduce-scatter.4.cloned.1.call-done = f32[16,1024]{1,0:T(8,128)} async-done(((f32[1024,1024]{1,0:T(8,128)}), f32[16,1024]{1,0:T(8,128)}) %reduce-scatter.4.cloned.1.call-update) | async-done | bytes 65552 | tf_op jit(solution)/shard_map/reduce_scatter | solution.py:117
  339.3 29.8 %all-gather = f32[128,1024]{1,0:T(8,128)S(1)} all-gather(f32[16,1024]{1,0:T(8,128)} %reduce-scatter.4.cloned.1.call-done), channel_id=2, replica_groups=mesh['dp'=8,'ctx'=64] {'dp'}, dimensions={0}, use_global_device_ids=true | all-gather | bytes 589824 | tf_op jit(solution)/shard_map/all_gather | solution.py:118
  369.1 0.6 fusion.177
  (90 shorter events, 4.9 us)
Async XLA Ops:
  7.2 1.3 copy-start
  7.2 31.8 %copy-start.8 = (bf16[1,256,512]{2,1,0:T(8,128)(2,1)S(1)}, bf16[1,256,512]{2,1,0:T(8,128)(2,1)}, u32[]{:S(2)}) copy-start(bf16[1,256,512]{2,1,0:T(8,128)(2,1)} %param.12) | copy-start | bytes 786436
  7.2 25.8 %copy-start.7 = (bf16[1,256,512]{2,1,0:T(8,128)(2,1)S(1)}, bf16[1,256,512]{2,1,0:T(8,128)(2,1)}, u32[]{:S(2)}) copy-start(bf16[1,256,512]{2,1,0:T(8,128)(2,1)} %param.11) | copy-start | bytes 786436
  7.2 33.0 %copy-start.26 = (s32[1,128]{1,0:T(1,128)S(1)}, s32[1,128]{1,0:T(1,128)}, u32[]{:S(2)}) copy-start(s32[1,128]{1,0:T(1,128)} %param.15) | copy-start | bytes 1540
  7.2 33.4 %copy-start.27 = (s32[1,32]{1,0:T(1,128)S(1)}, s32[1,32]{1,0:T(1,128)}, u32[]{:S(2)}) copy-start(s32[1,32]{1,0:T(1,128)} %param.13) | copy-start | bytes 388
  7.2 332.0 %reduce-scatter.4.cloned.1.call-start = ((), (), s32[]{:S(2)}) async-start(), calls=%async_computation.1 | async-start | bytes 4259840 | tf_op jit(solution)/shard_map/reduce_scatter | solution.py:117
  11.0 34.9 %collective-permute-start.5 = (bf16[256,1024]{1,0:T(8,128)(2,1)S(1)}, bf16[256,1024]{1,0:T(8,128)(2,1)}, u32[]{:S(2)}, u32[]{:S(2)}) collective-permute-start(bf16[256,1024]{1,0:T(8,128)(2,1)S(1)} %pad_maximum_fusion.1), channel_id=1, source_target_pairs={{0,61},{1,62},{2,63},{3,0},{4,1},{5,2},{6,3},{7,4},{8,5},{9,6},{10... | collective-permute-start | bytes 1572872 | tf_op jit(solution)/shard_map/ppermute | solution.py:15
  21.8 27.9 %collective-permute-start.4 = (bf16[256,1024]{1,0:T(8,128)(2,1)S(1)}, bf16[256,1024]{1,0:T(8,128)(2,1)}, u32[]{:S(2)}, u32[]{:S(2)}) collective-permute-start(bf16[256,1024]{1,0:T(8,128)(2,1)S(1)} %pad_maximum_fusion.1), channel_id=1, source_target_pairs={{0,62},{1,63},{2,0},{3,1},{4,2},{5,3},{6,4},{7,5},{8,6},{9,7},{10,... | collective-permute-start | bytes 1572872 | tf_op jit(solution)/shard_map/ppermute | solution.py:15
  26.3 25.3 %collective-permute-start.3 = (bf16[256,1024]{1,0:T(8,128)(2,1)S(1)}, bf16[256,1024]{1,0:T(8,128)(2,1)}, u32[]{:S(2)}, u32[]{:S(2)}) collective-permute-start(bf16[256,1024]{1,0:T(8,128)(2,1)S(1)} %pad_maximum_fusion.1), channel_id=1, source_target_pairs={{0,63},{1,0},{2,1},{3,2},{4,3},{5,4},{6,5},{7,6},{8,7},{9,8},{10,9... | collective-permute-start | bytes 1572872 | tf_op jit(solution)/shard_map/ppermute | solution.py:15
  33.9 21.8 %collective-permute-start.2 = (bf16[256,1024]{1,0:T(8,128)(2,1)}, bf16[256,1024]{1,0:T(8,128)(2,1)}, u32[]{:S(2)}, u32[]{:S(2)}) collective-permute-start(bf16[256,1024]{1,0:T(8,128)(2,1)} %pad_maximum_fusion), channel_id=1, source_target_pairs={{0,3},{1,4},{2,5},{3,6},{4,7},{5,8},{6,9},{7,10},{8,11},{9,12},{10... | collective-permute-start | bytes 1572872 | tf_op jit(solution)/shard_map/ppermute | solution.py:15
  35.8 30.1 %collective-permute-start.1 = (bf16[256,1024]{1,0:T(8,128)(2,1)}, bf16[256,1024]{1,0:T(8,128)(2,1)}, u32[]{:S(2)}, u32[]{:S(2)}) collective-permute-start(bf16[256,1024]{1,0:T(8,128)(2,1)} %pad_maximum_fusion), channel_id=1, source_target_pairs={{0,2},{1,3},{2,4},{3,5},{4,6},{5,7},{6,8},{7,9},{8,10},{9,11},{10,... | collective-permute-start | bytes 1572872 | tf_op jit(solution)/shard_map/ppermute | solution.py:15
  45.9 23.7 %collective-permute-start = (bf16[256,1024]{1,0:T(8,128)(2,1)}, bf16[256,1024]{1,0:T(8,128)(2,1)}, u32[]{:S(2)}, u32[]{:S(2)}) collective-permute-start(bf16[256,1024]{1,0:T(8,128)(2,1)} %pad_maximum_fusion), channel_id=1, source_target_pairs={{0,1},{1,2},{2,3},{3,4},{4,5},{5,6},{6,7},{7,8},{8,9},{9,10},{10,1... | collective-permute-start | bytes 1572872 | tf_op jit(solution)/shard_map/ppermute | solution.py:15
  82.7 4.2 %copy-start.16 = (f32[256,256]{1,0:T(8,128)S(1)}, f32[256,256]{1,0:T(8,128)}, u32[]{:S(2)}) copy-start(f32[256,256]{1,0:T(8,128)} %get-tuple-element.47) | copy-start | bytes 786436
  86.9 2.9 copy-start.9
  89.8 3.0 copy-start.11
  89.8 3.0 copy-start.13
  92.8 2.9 copy-start.10
  95.7 3.2 copy-start.12
  98.9 3.2 copy-start.1
  111.1 1.5 copy-start.20
  111.1 1.5 copy-start.23
  111.1 3.3 copy-start.6
  111.1 3.3 copy-start.19
  111.1 3.3 copy-start.24
  112.6 2.3 copy-start.5
  112.6 2.3 copy-start.18
  112.6 2.3 copy-start.25
  114.9 1.3 copy-start.4
  115.4 2.6 copy-start.3
  116.2 1.7 copy-start.17
  116.2 1.7 copy-start.21
  116.3 2.2 copy-start.2
  116.3 2.2 copy-start.14
  116.3 2.2 copy-start.15
  116.3 2.2 copy-start.22
Sparse Core Ops, SparseCore 0:
  111.2 227.9 reduce-scatter.3
